TPU v7x, 32 devices: a whole 2x2x4 slice. The times are simulated.
32 devices in a mesh: subj: 2 (over x), row: 8 (over z, y), col: 2 (over core).
Axes of the slice: x: 2, y: 2, z: 4, core: 2. Of those that a mesh axis runs over, the one named last changes fastest.
Arguments:
- series: float32 [256, 11392], P(('subj', 'row', 'col')), parts along dimension 0, may hold values from -30 to 30
- tap_values: float32 [17], replicated, may hold values from -4 to 4
- tap_count: int32 [1], replicated, may hold values from 4 to 8
- kept_frames: int32 [32], P('subj'), parts along dimension 0, may hold values from 1 to 8, 96 in all
- band_start: int32 [2], P('subj'), parts along dimension 0, may hold values from 0 to 7296
Outputs:
- fisher_band: bfloat16 [8192, 11392], P('subj', ('row', 'col')), parts along dimension 0
There are 2 independent parts, one for each index of `subj`. A program takes and returns all parts, laid end to end along the dimension named above; an argument that names none is the same for every part. Nothing has to cross between parts.
Inputs may be any that keep to these rules, and one draw needn't show every extreme that they name: `tap_count`: frames farther than this from the centre get no weight. Time block d holds frames d * 8 to (d + 1) * 8 - 1; only its first kept_frames[d] frames are kept. `band_start`: the 4096 band grayordinates lie inside the grid.
All inputs are finite; a program needn't handle non-finite values.
Results may differ from a plain program's by a relative error of at most 0.0031.
The roundings to bfloat16 on the way count: a program that leaves them out, or rounds other values in their place, can miss the bound.
Values may be sent and summed in bfloat16 or wider, within the bound.
No kernel may reach another device: no remote copies, remote signals or barrier semaphores. Data moves between devices by JAX's collectives and lax.ppermute only.
A program may use at most 128 MiB of HBM per device.

v0:
```python
import jax
import jax.numpy as jnp
from jax import lax
from jax.sharding import PartitionSpec as P

B = 4096
EPSILON = 1e-06
CLIP_LIMIT = 0.999


def with_halo(cells, sides, width):
    for axis, dim in sides:
        count = lax.axis_size(axis)
        ends = count - 1
        head = lax.slice_in_dim(cells, 0, width, axis=dim)
        tail = lax.slice_in_dim(cells, cells.shape[dim] - width, cells.shape[dim], axis=dim)
        cells = jnp.concatenate(
            [
                lax.ppermute(tail, axis, [(i, (i + 1) % count) for i in range(ends)]),
                cells,
                lax.ppermute(head, axis, [((i + 1) % count, i) for i in range(ends)]),
            ],
            axis=dim,
        )
    return cells


def tap_table(tap_values, tap_count):
    tap_reach = tap_values.shape[0] // 2
    offsets = jnp.arange(tap_values.shape[0], dtype=jnp.int32) - tap_reach
    active = (jnp.abs(offsets) <= tap_count[0]).astype(jnp.float32)
    centre = jnp.sum(active * tap_values) / jnp.sum(active)
    return active * (tap_values - centre)


def band_filter(padded, tap_weights, length):
    filtered = tap_weights[0] * padded[0:length]
    for tap_index in range(1, tap_weights.shape[0]):
        filtered = filtered + tap_weights[tap_index] * padded[tap_index : tap_index + length]
    return filtered


def fisher_z(correlation):
    clipped = jnp.clip(correlation, -CLIP_LIMIT, CLIP_LIMIT)
    return 0.5 * (jnp.log1p(clipped) - jnp.log1p(-clipped))


def body(series, tap_values, tap_count, kept_frames, band_start):
    tap_reach = tap_values.shape[0] // 2
    tap_weights = tap_table(tap_values, tap_count)
    block_len = series.shape[0]
    padded = with_halo(series, ((("row", "col"), 0),), tap_reach)
    filtered = band_filter(padded, tap_weights, block_len)
    own_kept = kept_frames[lax.axis_index(("row", "col"))]
    keep_mask = (jnp.arange(block_len, dtype=jnp.int32) < own_kept).astype(jnp.float32)[:, None]
    centered = keep_mask * filtered
    spread = lax.psum(jnp.sum(centered * centered, axis=0), ("row", "col"))
    scaled = (centered * lax.rsqrt(spread + EPSILON)).astype(jnp.bfloat16)
    columns = lax.all_to_all(scaled, ("row", "col"), split_axis=1, concat_axis=0, tiled=True)
    band_slice = lax.dynamic_slice_in_dim(scaled, band_start[0], B, 1)
    band_cols = lax.all_gather(band_slice, ("row", "col"), axis=0, tiled=True)
    correlation = lax.dot_general(
        band_cols, columns, (((0,), (0,)), ((), ())), preferred_element_type=jnp.float32
    )
    return fisher_z(correlation).astype(jnp.bfloat16)


def solution(mesh):
    placed = (P(("subj", "row", "col"), None), P(), P(), P("subj"), P("subj"))
    return jax.shard_map(
        body, mesh=mesh, in_specs=placed, out_specs=P("subj", ("row", "col")), check_vma=False
    )
```

profile of v0, /device:TPU:0, one launch (start us, length us, event | category | flops | bytes accessed | tf_op | source)
XLA Modules:
  0.0 151.6 jit_solution(5790544908060387476)
XLA Ops:
  6.5 0.0 all-gather.2.cloned.1.call-start
  6.5 2.4 %collective-permute-start = (f32[8,11392]{1,0:T(8,128)}, f32[8,11392]{1,0:T(8,128)S(1)}, u32[]{:S(2)}, u32[]{:S(2)}) collective-permute-start(f32[8,11392]{1,0:T(8,128)} %param.5), channel_id=1, source_target_pairs={{0,1},{1,2},{2,3},{3,4},{4,5},{5,6},{6,7},{7,8},{8,9},{9,10},{10,1... | collective-permute-start | bytes 1093640 | tf_op jit(solution)/shard_map/ppermute | solution.py:19
  8.9 1.3 collective-permute-start.1
  10.9 1.3 dynamic_slice.6
  12.1 1.3 convert_reduce_fusion
  13.5 0.6 compare_convert_fusion
  16.1 0.7 subtract_select_fusion
  16.7 0.7 fusion.19
  17.4 0.0 collective-permute-done
  17.5 1.0 constant_dynamic-update-slice_fusion
  18.5 0.0 collective-permute-done.1
  18.6 12.4 %multiply_reduce_fusion = (f32[11392]{0:T(1024)S(1)}, f32[8,11392]{1,0:T(8,128)S(1)}) fusion(f32[8,11392]{1,0:T(8,128)S(1)} %collective-permute-done.1, f32[]{:T(128)} %bitcast.18, f32[16,11392]{1,0:T(8,128)S(1)} %constant_dynamic-update-slice_fusion.2, f32[]{:T(128)} %bitcast.17, f32[]{:T(128)} %bitcast.16, f32[]{:T(128)} %bitcast.15, f32[]{:T(128)} %bitcast.14, ...), kind=kLoop, calls=%fused_computation.33 | loop fusion | flops 3269504 | bytes 6607460 | tf_op jit(solution)/shard_map/reduce_sum | solution.py:57
  31.0 63.9 %psum.7 = f32[11392]{0:T(1024)S(1)} all-reduce(f32[11392]{0:T(1024)S(1)} %get-tuple-element.5), channel_id=1, replica_groups=mesh['subj'=2,'row'=8,'col'=2] {'row','col'}, use_global_device_ids=true, to_apply=%region_3.0 | all-reduce | flops 11392 | bytes 91136 | tf_op jit(solution)/shard_map/psum | solution.py:57
  94.9 0.7 constant_dynamic-slice_fusion
  95.7 0.0 all-gather.2.cloned.1.call-update
  95.7 0.4 all_to_all.14
  96.1 0.1 copy.6
  96.2 12.3 %all_to_all.19 = bf16[8,16,712]{2,0,1:T(8,128)(2,1)S(1)} all-to-all(bf16[8,16,712]{2,0,1:T(8,128)(2,1)S(1)} %copy.6), channel_id=1, replica_groups=mesh['subj'=2,'row'=8,'col'=2] {'row','col'}, dimensions={1} | all-to-all | bytes 364544 | tf_op jit(solution)/shard_map/all_to_all | solution.py:59
  108.5 23.6 %all-gather.2.cloned.1.call-done = bf16[128,4096]{1,0:T(8,128)(2,1)} async-done(((bf16[8,4096]{1,0:T(8,128)(2,1)}), bf16[128,4096]{1,0:T(8,128)(2,1)}) %all-gather.2.cloned.1.call-update) | async-done | bytes 1048592 | tf_op jit(solution)/shard_map/all_gather | solution.py:61
  132.1 12.7 %multiply_convert_fusion = bf16[4096,712]{0,1:T(8,128)(2,1)} fusion(bf16[128,4096]{1,0:T(8,128)(2,1)} %all-gather.2.cloned.1.call-done, bf16[8,16,712]{2,0,1:T(8,128)(2,1)S(1)} %all_to_all.19), kind=kOutput, calls=%fused_computation | convolution fusion | flops 761167872 | bytes 7063552 | tf_op jit(solution)/shard_map/dot_general | solution.py:62
  (4 shorter events, 0.1 us)
Async XLA Ops:
  6.5 125.6 %all-gather.2.cloned.1.call-start = ((), (), s32[]{:S(2)}) async-start(), calls=%async_computation.1 | async-start | bytes 1114112 | tf_op jit(solution)/shard_map/all_gather | solution.py:61
  6.5 10.9 %collective-permute-start = (f32[8,11392]{1,0:T(8,128)}, f32[8,11392]{1,0:T(8,128)S(1)}, u32[]{:S(2)}, u32[]{:S(2)}) collective-permute-start(f32[8,11392]{1,0:T(8,128)} %param.5), channel_id=1, source_target_pairs={{0,1},{1,2},{2,3},{3,4},{4,5},{5,6},{6,7},{7,8},{8,9},{9,10},{10,1... | collective-permute-start | bytes 1093640 | tf_op jit(solution)/shard_map/ppermute | solution.py:19
  8.9 9.6 %collective-permute-start.1 = (f32[8,11392]{1,0:T(8,128)}, f32[8,11392]{1,0:T(8,128)S(1)}, u32[]{:S(2)}, u32[]{:S(2)}) collective-permute-start(f32[8,11392]{1,0:T(8,128)} %param.5), channel_id=1, source_target_pairs={{1,0},{2,1},{3,2},{4,3},{5,4},{6,5},{7,6},{8,7},{9,8},{10,9},{11,1... | collective-permute-start | bytes 1093640 | tf_op jit(solution)/shard_map/ppermute | solution.py:21
Sparse Core Ops, SparseCore 0:
  95.8 36.2 all-gather.1
where the time goes:
time: 152 us
  blocking collectives  76.2 us (50%)
  waiting for transfers between devices  23.6 us (16%)
  between operations  16.1 us (11%)
  other arithmetic  15.1 us (10%)
  matrix products  12.7 us (8%)
  local copies, waits for them, and re-layouts  4.28 us (3%)
  starting transfers between devices  3.66 us (2%)
    psum x1, blocking collectives, body(): spread = lax.psum(jnp.sum(centered * centered, axis=0), ('row', 'col'))  63.9 us
    all_gather x1, waiting for transfers between devices, body(): band_cols = lax.all_gather(band_slice, ('row', 'col'), axis=0, tiled=True)  23.6 us
    dot_general x1, matrix products, body(): lax.dot_general(band_cols, columns, (((0,), (0,)), ((), ())), preferred_e...  12.7 us
    reduce_sum x1, other arithmetic, body(): spread = lax.psum(jnp.sum(centered * centered, axis=0), ('row', 'col'))  12.4 us
    all_to_all x1, blocking collectives, body(): lax.all_to_all(scaled, ('row', 'col'), split_axis=1, concat_axis=0, tiled...  12.3 us
  transfers between devices with their start and end apart: 3, of which 1 were waited for; matrix products, arithmetic and copies ran while one was open for 4% of the time, Pallas kernels for 0%

commit v1 on v0

--- a/solution.py
+++ b/solution.py
@@ -54,7 +54,7 @@
     own_kept = kept_frames[lax.axis_index(("row", "col"))]
     keep_mask = (jnp.arange(block_len, dtype=jnp.int32) < own_kept).astype(jnp.float32)[:, None]
     centered = keep_mask * filtered
-    spread = lax.psum(jnp.sum(centered * centered, axis=0), ("row", "col"))
+    spread = jnp.sum(lax.all_gather(jnp.sum(centered * centered, axis=0), ("row", "col")), axis=0)
     scaled = (centered * lax.rsqrt(spread + EPSILON)).astype(jnp.bfloat16)
     columns = lax.all_to_all(scaled, ("row", "col"), split_axis=1, concat_axis=0, tiled=True)
     band_slice = lax.dynamic_slice_in_dim(scaled, band_start[0], B, 1)

time: 152 us -> 116 us (0.76)
  blocking collectives: 76.2 us -> 39.3 us
    psum x1 -> x0, blocking collectives: 63.9 us -> none  [body(): spread = lax.psum(jnp.sum(centered * centered, axis=0), ('row', 'col'))]
    all_gather x0 -> x1, blocking collectives: none -> 27 us  [body(): lax.all_gather(jnp.sum(centered * centered, axis=0), ('row', 'col'))]
    reduce_sum x1 -> x2, other arithmetic: 12.4 us -> 12.8 us  [the longest x1 12.4 us: body(): jnp.sum(centered * centered, axis=0)]
  transfers between devices with their start and end apart: 3 -> 3, of which waited for: 1 -> 1; matrix products, arithmetic and copies ran while one was open for 4% -> 5% of each run, Pallas kernels for 0% -> 0%
where the time goes in v1:
time: 116 us; the launch traced here: 115 us
  blocking collectives  39.3 us (34%)
  waiting for transfers between devices  23.7 us (20%)
  between operations  16.1 us (14%)
  other arithmetic  15.5 us (13%)
  matrix products  12.7 us (11%)
  local copies, waits for them, and re-layouts  4.31 us (4%)
  starting transfers between devices  3.66 us (3%)
    all_gather x1, blocking collectives, body(): lax.all_gather(jnp.sum(centered * centered, axis=0), ('row', 'col'))  27 us
    all_gather x1, waiting for transfers between devices, body(): band_cols = lax.all_gather(band_slice, ('row', 'col'), axis=0, tiled=True)  23.6 us
    dot_general x1, matrix products, body(): lax.dot_general(band_cols, columns, (((0,), (0,)), ((), ())), preferred_e...  12.7 us
    reduce_sum x1, other arithmetic, body(): jnp.sum(centered * centered, axis=0)  12.4 us
    all_to_all x1, blocking collectives, body(): lax.all_to_all(scaled, ('row', 'col'), split_axis=1, concat_axis=0, tiled...  12.3 us
    ppermute x1, starting transfers between devices, with_halo(): lax.ppermute(tail, axis, [(i, (i + 1) % count) for i in range(ends)])  2.37 us
  transfers between devices with their start and end apart: 3, of which 1 were waited for; matrix products, arithmetic and copies ran while one was open for 5% of the time, Pallas kernels for 0%

profile of v1, /device:TPU:0, one launch (start us, length us, event | category | flops | bytes accessed | tf_op | source)
XLA Modules:
  0.0 115.2 jit_solution(9735757666128327765)
XLA Ops:
  6.5 0.0 all-gather.4.cloned.1.call-start
  6.5 2.4 %collective-permute-start = (f32[8,11392]{1,0:T(8,128)}, f32[8,11392]{1,0:T(8,128)S(1)}, u32[]{:S(2)}, u32[]{:S(2)}) collective-permute-start(f32[8,11392]{1,0:T(8,128)} %param.5), channel_id=1, source_target_pairs={{0,1},{1,2},{2,3},{3,4},{4,5},{5,6},{6,7},{7,8},{8,9},{9,10},{10,1... | collective-permute-start | bytes 1093640 | tf_op jit(solution)/shard_map/ppermute | solution.py:19
  8.9 1.3 %collective-permute-start.1 = (f32[8,11392]{1,0:T(8,128)}, f32[8,11392]{1,0:T(8,128)S(1)}, u32[]{:S(2)}, u32[]{:S(2)}) collective-permute-start(f32[8,11392]{1,0:T(8,128)} %param.5), channel_id=1, source_target_pairs={{1,0},{2,1},{3,2},{4,3},{5,4},{6,5},{7,6},{8,7},{9,8},{10,9},{11,1... | collective-permute-start | bytes 1093640 | tf_op jit(solution)/shard_map/ppermute | solution.py:21
  10.9 1.3 %dynamic_slice.6 = s32[1]{0:T(128)} dynamic-slice(s32[16]{0:T(128)} %param.8, s32[]{:T(128)S(6)} %select_n.6), dynamic_slice_sizes={1} | dynamic-slice | bytes 12 | tf_op jit(solution)/shard_map/dynamic_slice | solution.py:54
  12.1 1.3 %convert_reduce_fusion = (f32[]{:T(128)}, f32[]{:T(128)}) fusion(s32[]{:T(128)} %bitcast.26, f32[17]{0:T(128)} %param.6), kind=kLoop, calls=%fused_computation.42 | loop fusion | flops 117 | bytes 80 | tf_op jit(solution)/shard_map/reduce_sum | solution.py:32
  13.5 0.6 compare_convert_fusion
  16.1 0.7 subtract_select_fusion
  16.7 0.7 fusion.19
  17.4 0.0 collective-permute-done
  17.5 1.0 constant_dynamic-update-slice_fusion
  18.5 0.0 collective-permute-done.1
  18.6 12.4 %multiply_reduce_fusion = (f32[11392]{0:T(1024)S(1)}, f32[8,11392]{1,0:T(8,128)S(1)}) fusion(f32[8,11392]{1,0:T(8,128)S(1)} %collective-permute-done.1, f32[]{:T(128)} %bitcast.18, f32[16,11392]{1,0:T(8,128)S(1)} %constant_dynamic-update-slice_fusion.2, f32[]{:T(128)} %bitcast.17, f32[]{:T(128)} %bitcast.16, f32[]{:T(128)} %bitcast.15, f32[]{:T(128)} %bitcast.14, ...), kind=kLoop, calls=%fused_computation.33 | loop fusion | flops 3269504 | bytes 6607460 | tf_op jit(solution)/shard_map/reduce_sum | solution.py:57
  31.0 27.0 %all-gather.1 = f32[16,1,11392]{2,1,0:T(1,128)S(1)} all-gather(f32[1,1,11392]{2,1,0:T(1,128)S(1)} %reshape.13), channel_id=2, replica_groups=mesh['subj'=2,'row'=8,'col'=2] {'row','col'}, dimensions={0}, use_global_device_ids=true | all-gather | bytes 774656 | tf_op jit(solution)/shard_map/all_gather | solution.py:57
  58.0 0.5 reduce_sum.39
  58.5 0.7 constant_dynamic-slice_fusion
  59.2 0.0 all-gather.4.cloned.1.call-update
  59.3 0.4 all_to_all.14
  59.7 0.1 copy.7
  59.8 12.3 %all_to_all.19 = bf16[8,16,712]{2,0,1:T(8,128)(2,1)S(1)} all-to-all(bf16[8,16,712]{2,0,1:T(8,128)(2,1)S(1)} %copy.7), channel_id=1, replica_groups=mesh['subj'=2,'row'=8,'col'=2] {'row','col'}, dimensions={1} | all-to-all | bytes 364544 | tf_op jit(solution)/shard_map/all_to_all | solution.py:59
  72.1 23.6 %all-gather.4.cloned.1.call-done = bf16[128,4096]{1,0:T(8,128)(2,1)} async-done(((bf16[8,4096]{1,0:T(8,128)(2,1)}), bf16[128,4096]{1,0:T(8,128)(2,1)}) %all-gather.4.cloned.1.call-update) | async-done | bytes 1048592 | tf_op jit(solution)/shard_map/all_gather | solution.py:61
  95.7 12.7 %multiply_convert_fusion = bf16[4096,712]{0,1:T(8,128)(2,1)} fusion(bf16[128,4096]{1,0:T(8,128)(2,1)} %all-gather.4.cloned.1.call-done, bf16[8,16,712]{2,0,1:T(8,128)(2,1)S(1)} %all_to_all.19), kind=kOutput, calls=%fused_computation | convolution fusion | flops 761167872 | bytes 7063552 | tf_op jit(solution)/shard_map/dot_general | solution.py:62
  (5 shorter events, 0.1 us)
Async XLA Ops:
  6.5 89.2 %all-gather.4.cloned.1.call-start = ((), (), s32[]{:S(2)}) async-start(), calls=%async_computation.1 | async-start | bytes 1114112 | tf_op jit(solution)/shard_map/all_gather | solution.py:61
  6.5 10.9 %collective-permute-start = (f32[8,11392]{1,0:T(8,128)}, f32[8,11392]{1,0:T(8,128)S(1)}, u32[]{:S(2)}, u32[]{:S(2)}) collective-permute-start(f32[8,11392]{1,0:T(8,128)} %param.5), channel_id=1, source_target_pairs={{0,1},{1,2},{2,3},{3,4},{4,5},{5,6},{6,7},{7,8},{8,9},{9,10},{10,1... | collective-permute-start | bytes 1093640 | tf_op jit(solution)/shard_map/ppermute | solution.py:19
  8.9 9.6 %collective-permute-start.1 = (f32[8,11392]{1,0:T(8,128)}, f32[8,11392]{1,0:T(8,128)S(1)}, u32[]{:S(2)}, u32[]{:S(2)}) collective-permute-start(f32[8,11392]{1,0:T(8,128)} %param.5), channel_id=1, source_target_pairs={{1,0},{2,1},{3,2},{4,3},{5,4},{6,5},{7,6},{8,7},{9,8},{10,9},{11,1... | collective-permute-start | bytes 1093640 | tf_op jit(solution)/shard_map/ppermute | solution.py:21
Sparse Core Ops, SparseCore 0:
  59.4 36.2 all-gather.3
